TPU v7x, 32 devices: a whole 2x2x4 slice. The times are simulated.
32 devices in a mesh: blk: 8 (over z, y), lblk: 4 (over x, core).
Axes of the slice: x: 2, y: 2, z: 4, core: 2. Of those that a mesh axis runs over, the one named last changes fastest.
Arguments:
- sky: bfloat16 [8, 2, 32, 16384], P(None, None, 'blk', 'lblk'), may hold values from -6 to 6
- arc_start: int32 [2, 32], P(None, 'blk'), may hold values from 0 to 16383
- arc_count: int32 [2, 32], P(None, 'blk'), may hold values from 4096 to 16384
- owner_modes: int32 [32], replicated, may hold values from 0 to 31, each once
- legendre: bfloat16 [32, 8, 4, 4096], P('blk', None, None, 'lblk'), may hold values from -1 to 1
Outputs:
- alm: float32 [8, 2, 32, 4096], P(None, None, 'blk', 'lblk')
Inputs may be any that keep to these rules, and one draw needn't show every extreme that they name: `owner_modes`: each m-mode 0 to 31 appears exactly once.
All inputs are finite; a program needn't handle non-finite values.
Results may differ from a plain program's by a relative error of at most 0.0049.
Values may be sent and summed in bfloat16 or wider, within the bound.
No kernel may reach another device: no remote copies, remote signals or barrier semaphores. Data moves between devices by JAX's collectives and lax.ppermute only.
A program may use at most 64 MiB of HBM per device.

v0:
```python
import math
import jax
import jax.numpy as jnp
from jax import lax
from jax.sharding import PartitionSpec as P

RLEN = 16384
DIFFUSION = 0.2


def padded(x, sides, width, wrap):
    for axis, dim in sides:
        count, length = (lax.axis_size(axis), x.shape[dim])
        up = [(i, (i + 1) % count) for i in range(count if wrap else count - 1)]
        down = [(j, i) for i, j in up]
        last = lax.slice_in_dim(x, length - width, length, axis=dim)
        initial = lax.slice_in_dim(x, 0, width, axis=dim)
        before = lax.ppermute(last, axis, up)
        after = lax.ppermute(initial, axis, down)
        x = jnp.concatenate([before, x, after], axis=dim)
    return x


def mode_basis(positions, mode_list):
    product_index = jnp.mod(positions[:, None] * mode_list[None, :], RLEN)
    angles = 2.0 * math.pi / RLEN * product_index.astype(jnp.float32)
    return (jnp.cos(angles).astype(jnp.bfloat16), (-jnp.sin(angles)).astype(jnp.bfloat16))


def legendre_section(fourier, legendre_rows, my_modes, degrees):
    north_part = fourier[:, 0].astype(jnp.float32)
    south_part = fourier[:, 1].astype(jnp.float32)
    folded = jnp.concatenate([north_part + south_part, north_part - south_part], axis=2).astype(
        jnp.bfloat16
    )
    latitude_sums = jnp.einsum(
        "xrys,srl->xysl", folded, legendre_rows, preferred_element_type=jnp.float32
    )
    even_parity = jnp.mod(degrees[None, :] + my_modes[:, None], 2) == 0
    chosen = jnp.where(even_parity[None, None], latitude_sums[:, :2], latitude_sums[:, 2:])
    inside = (degrees[None, :] >= my_modes[:, None])[None, None]
    return jnp.where(inside, chosen, jnp.zeros((), jnp.float32))


def local(sky, arc_start, arc_count, owner_modes, legendre):
    maps_here = sky.shape[0]
    band_here = sky.shape[2]
    quarter = sky.shape[3]
    column = lax.axis_index("lblk")
    positions = column * quarter + jnp.arange(quarter, dtype=jnp.int32)
    offset = jnp.mod(positions[None, None, :] - arc_start[:, :, None], RLEN)
    kept_mask = offset < arc_count[:, :, None]
    masked = jnp.where(kept_mask[None], sky, jnp.zeros((), jnp.bfloat16))
    layered = padded(masked, (("blk", 2),), 1, False)
    edge_padded = padded(masked, (("lblk", 3),), 1, True)
    is_last = lax.axis_index("blk") == lax.axis_size("blk") - 1
    beyond = jnp.where(is_last, masked[:, ::-1, band_here - 1 :], layered[:, :, band_here + 1 :])
    centre = masked.astype(jnp.float32)
    layer_above = layered[:, :, :band_here].astype(jnp.float32)
    layer_below = jnp.concatenate([layered[:, :, 2 : band_here + 1], beyond], axis=2).astype(
        jnp.float32
    )
    pixel_before = edge_padded[:, :, :, :quarter].astype(jnp.float32)
    pixel_after = edge_padded[:, :, :, 2:].astype(jnp.float32)
    total = layer_above + layer_below + pixel_before + pixel_after - 4.0 * centre
    smooth = (centre + DIFFUSION * total).astype(jnp.bfloat16)
    cos_table, sin_table = mode_basis(positions, owner_modes)
    slab_size = owner_modes.shape[0]
    flat_rows = smooth.reshape(maps_here * 2 * band_here, quarter)
    real_part = jnp.dot(flat_rows, cos_table, preferred_element_type=jnp.float32).reshape(
        maps_here, 2, band_here, slab_size
    )
    imag_part = jnp.dot(flat_rows, sin_table, preferred_element_type=jnp.float32).reshape(
        maps_here, 2, band_here, slab_size
    )
    parity = jnp.arange(band_here, dtype=jnp.int32) % 2
    phase_turn = math.pi / RLEN * (parity[:, None] * owner_modes[None, :]).astype(jnp.float32)
    turn_cos = jnp.cos(phase_turn)
    turn_sin = jnp.sin(phase_turn)
    norm_scale = 1.0 / math.sqrt(RLEN)
    rotated_real = (real_part * turn_cos + imag_part * turn_sin) * norm_scale
    rotated_imag = (imag_part * turn_cos - real_part * turn_sin) * norm_scale
    partial_value = jnp.stack([rotated_real, rotated_imag], axis=3)
    owned_count = legendre.shape[0]
    degree_part = legendre.shape[3]
    my_modes = lax.dynamic_slice_in_dim(
        owner_modes, lax.axis_index("blk") * owned_count, owned_count
    )
    degrees = column * degree_part + jnp.arange(degree_part, dtype=jnp.int32)
    legendre_rows = legendre.reshape(owned_count, -1, degree_part)
    spread = lax.all_to_all(partial_value, "blk", split_axis=4, concat_axis=2, tiled=True)
    summed = lax.psum(spread, "lblk")
    fourier = summed.astype(jnp.bfloat16)
    result = legendre_section(fourier, legendre_rows, my_modes, degrees)
    return result


def solution(mesh):
    return jax.shard_map(
        local,
        mesh=mesh,
        in_specs=(
            P(None, None, "blk", "lblk"),
            P(None, "blk"),
            P(None, "blk"),
            P(),
            P("blk", None, None, "lblk"),
        ),
        out_specs=P(None, None, "blk", "lblk"),
        check_vma=False,
    )
```

profile of v0, /device:TPU:0, one launch (start us, length us, event | category | flops | bytes accessed | tf_op | source)
XLA Modules:
  0.0 53.8 jit_solution(13409327666316147105)
XLA Ops:
  0.0 0.0 copy-start.1
  0.0 0.0 copy-start.2
  0.0 0.7 %copy-done.1 = s32[2,4]{1,0:T(2,128)S(1)} copy-done((s32[2,4]{1,0:T(2,128)S(1)}, s32[2,4]{1,0:T(2,128)}, u32[]{:S(2)}) %copy-start.1) | copy-done | bytes 56
  0.7 0.0 copy-done.2
  0.7 0.2 fusion.16
  0.9 1.3 %broadcast_select_fusion.1 = bf16[8,2,4,4096]{3,2,1,0:T(4,128)(2,1)S(1)} fusion(bf16[8,2,4,4096]{3,2,1,0:T(4,128)(2,1)} %param.5, pred[2,4,4096]{2,1,0:T(4,128)(4,1)S(1)} %fusion.16), kind=kLoop, calls=%fused_computation.20 | loop fusion | flops 262144 | bytes 1081344 | tf_op jit(solution)/shard_map/jit(_where)/select_n | solution.py:53
  2.2 0.6 %fusion.38 = (bf16[8,2,1,4096]{3,2,1,0:T(2,128)(2,1)S(1)}, bf16[8,2,1,4096]{3,2,1,0:T(2,128)(2,1)S(1)}) fusion(bf16[8,2,4,4096]{3,2,1,0:T(4,128)(2,1)S(1)} %broadcast_select_fusion.1), kind=kLoop, calls=%fused_computation.70 | loop fusion | bytes 524288 | tf_op jit(solution)/shard_map/slice | solution.py:17
  2.8 1.3 %collective-permute-start.1 = (bf16[8,2,1,4096]{3,2,1,0:T(2,128)(2,1)S(1)}, bf16[8,2,1,4096]{3,2,1,0:T(2,128)(2,1)S(1)}, u32[]{:S(2)}, u32[]{:S(2)}) collective-permute-start(bf16[8,2,1,4096]{3,2,1,0:T(2,128)(2,1)S(1)} %get-tuple-element.5), channel_id=1, source_target_pairs={{4,0},{8,4},{12,8},{16,12},{20,16},{24,20},{28,24},{5,1},{9,5},{13... | collective-permute-start | bytes 393224 | tf_op jit(solution)/shard_map/ppermute | solution.py:19
  4.1 5.5 %collective-permute-start = (bf16[8,2,1,4096]{3,2,1,0:T(2,128)(2,1)S(1)}, bf16[8,2,1,4096]{3,2,1,0:T(2,128)(2,1)S(1)}, u32[]{:S(2)}, u32[]{:S(2)}) collective-permute-start(bf16[8,2,1,4096]{3,2,1,0:T(2,128)(2,1)S(1)} %get-tuple-element.6), channel_id=1, source_target_pairs={{0,4},{4,8},{8,12},{12,16},{16,20},{20,24},{24,28},{1,5},{5,9},{9,... | collective-permute-start | bytes 393224 | tf_op jit(solution)/shard_map/ppermute | solution.py:18
  9.6 0.1 fusion.39
  9.7 0.1 collective-permute-start.2
  9.8 0.0 copy-start.3
  9.8 1.7 %collective-permute-start.3 = (bf16[8,2,4,1]{3,2,1,0:T(4,128)(2,1)S(1)}, bf16[8,2,4,1]{3,2,1,0:T(4,128)(2,1)S(1)}, u32[]{:S(2)}, u32[]{:S(2)}) collective-permute-start(bf16[8,2,4,1]{3,2,1,0:T(4,128)(2,1)S(1)} %get-tuple-element.8), channel_id=1, source_target_pairs={{1,0},{2,1},{3,2},{0,3},{5,4},{6,5},{7,6},{4,7},{9,8},{10,9},{11,1... | collective-permute-start | bytes 392 | tf_op jit(solution)/shard_map/ppermute | solution.py:19
  11.5 0.0 copy-done.3
  11.5 0.1 fusion.28
  11.6 0.3 slice.52
  11.9 0.1 dynamic_slice.3
  12.0 2.0 %collective-permute-done.1 = bf16[8,2,1,4096]{3,2,1,0:T(2,128)(2,1)S(1)} collective-permute-done((bf16[8,2,1,4096]{3,2,1,0:T(2,128)(2,1)S(1)}, bf16[8,2,1,4096]{3,2,1,0:T(2,128)(2,1)S(1)}, u32[]{:S(2)}, u32[]{:S(2)}) %collective-permute-start.1) | collective-permute-done | bytes 131104 | tf_op jit(solution)/shard_map/ppermute | solution.py:19
  14.0 0.4 broadcast_select_fusion
  14.4 0.0 collective-permute-done.2
  14.4 0.0 collective-permute-done.3
  14.4 5.3 %collective-permute-done = bf16[8,2,1,4096]{3,2,1,0:T(2,128)(2,1)S(1)} collective-permute-done((bf16[8,2,1,4096]{3,2,1,0:T(2,128)(2,1)S(1)}, bf16[8,2,1,4096]{3,2,1,0:T(2,128)(2,1)S(1)}, u32[]{:S(2)}, u32[]{:S(2)}) %collective-permute-start) | collective-permute-done | bytes 131104 | tf_op jit(solution)/shard_map/ppermute | solution.py:18
  19.7 2.3 %fusion.2 = bf16[8,2,4,4096]{3,2,1,0:T(4,128)(2,1)S(1)} fusion(bf16[8,2,4,4096]{3,2,1,0:T(4,128)(2,1)S(1)} %broadcast_select_fusion.1, bf16[8,2,4,1]{3,2,1,0:T(4,128)(2,1)S(1)} %collective-permute-done.3, bf16[8,2,4,1]{3,2,1,0:T(4,128)(2,1)S(1)} %collective-permute-done.2, bf16[8,2,1,4096]{3,2,1,0:T(2,128)(2,1)S(1)} %collective-permute-done, ...), kind=kLoop, calls=%fused_computation.5 | loop fusion | flops 6553600 | bytes 1704192 | tf_op jit(solution)/shard_map/convert_element_type | solution.py:66
  22.0 2.2 %fusion.7 = f32[8,2,4,32]{3,2,1,0:T(4,128)S(1)} fusion(bf16[8,2,4,4096]{3,2,1,0:T(4,128)(2,1)S(1)} %fusion.2, s32[32]{0:T(128)S(1)} %copy-done.3, s32[4096]{0:T(1024)S(1)} %iota_add_fusion), kind=kOutput, calls=%fused_computation.22 | convolution fusion | flops 18743296 | bytes 548992 | tf_op jit(solution)/shard_map/dot_general | solution.py:70
  24.3 2.3 %multiply_bitcast_fusion.1 = (f32[8,2,4,1,32]{4,2,1,0,3:T(4,128)S(1)}, f32[8,2,4,1,32]{4,2,1,0,3:T(4,128)S(1)}) fusion(f32[8,2,4,32]{3,2,1,0:T(4,128)S(1)} %fusion.7, f32[4,32]{1,0:T(4,128)S(1)} %get-tuple-element.16, f32[4,32]{1,0:T(4,128)S(1)} %get-tuple-element.15, bf16[8,2,4,4096]{3,2,1,0:T(4,128)(2,1)S(1)} %fusion.2, s32[32]{0:T(128)S(1)} %copy-done.3, ...), kind=kOutput, calls=%fused_computation.44 | convolution fusion | flops 18890752 | bytes 566400 | tf_op jit(solution)/shard_map/dot_general | solution.py:73
  26.6 0.0 copy-start
  26.6 0.2 copy.16
  26.8 0.9 %reshape.175 = f32[8,1,512]{2,1,0:T(1,128)} reshape(f32[32,2,2,4,8]{4,3,2,1,0:T(4,128)S(1)} %bitcast.33) | data formatting | bytes 32768
  27.7 5.8 %all-to-all-start = ((f32[8,1,512]{2,1,0:T(1,128)}), f32[8,1,512]{2,1,0:T(1,128)S(1)}, u32[]{:S(2)}, u32[]{:S(2)}) async-start(f32[8,1,512]{2,1,0:T(1,128)} %reshape.175), calls=%async_computation | async-start | bytes 32768 | tf_op jit(solution)/shard_map/all_to_all | solution.py:91
  33.5 0.1 broadcast_compare_fusion
  33.6 0.0 copy-done
  33.6 0.1 reshape.173
  33.6 6.4 %all-to-all-done = f32[8,1,512]{2,1,0:T(1,128)S(1)} async-done(((f32[8,1,512]{2,1,0:T(1,128)}), f32[8,1,512]{2,1,0:T(1,128)S(1)}, u32[]{:S(2)}, u32[]{:S(2)}) %all-to-all-start) | async-done | bytes 16416 | tf_op jit(solution)/shard_map/all_to_all | solution.py:91
  40.0 0.5 broadcast.207
  40.5 0.7 %reduce = f32[8,512]{1,0:T(8,128)S(1)} reduce(f32[8,1,512]{2,1,0:T(1,128)S(1)} %all-to-all-done, f32[]{:T(128)} %broadcast.207), dimensions={1}, to_apply=%all_to_all.13.reduce_sub_computation | reduce | bytes 32772 | tf_op jit(solution)/shard_map/all_to_all | solution.py:91
  41.2 0.3 reshape.176
  41.6 0.1 copy.17
  41.7 0.2 copy.18
  41.9 0.1 copy.19
  42.0 10.7 %psum.7 = bf16[8,2,32,2,4]{2,0,3,4,1:T(8,128)(2,1)S(1)} all-reduce(f32[8,2,32,2,4]{2,0,3,4,1:T(8,128)S(1)} %copy.19), channel_id=1, replica_groups=mesh['blk'=8,'lblk'=4] {'lblk'}, use_global_device_ids=true, to_apply=%region_0.1 | all-reduce | flops 4096 | bytes 24576 | tf_op jit(solution)/shard_map/psum | solution.py:92
  52.7 0.2 convolution_bitcast_fusion
  52.9 0.1 fusion.12
  52.9 0.9 %copy.20 = f32[8,2,4,1024]{3,2,1,0:T(4,128)} copy(f32[8,2,4,1024]{3,0,1,2:T(8,128)S(1)} %fusion.12) | data formatting | bytes 524288 | tf_op jit(solution)/shard_map/jit(_where)/select_n | solution.py:42
  (5 shorter events, 0.0 us)
Async XLA Ops:
  0.0 0.7 %copy-start.1 = (s32[2,4]{1,0:T(2,128)S(1)}, s32[2,4]{1,0:T(2,128)}, u32[]{:S(2)}) copy-start(s32[2,4]{1,0:T(2,128)} %param.7) | copy-start | bytes 100
  0.0 0.7 %copy-start.2 = (s32[2,4]{1,0:T(2,128)S(1)}, s32[2,4]{1,0:T(2,128)}, u32[]{:S(2)}) copy-start(s32[2,4]{1,0:T(2,128)} %param.6) | copy-start | bytes 100
  2.8 11.2 %collective-permute-start.1 = (bf16[8,2,1,4096]{3,2,1,0:T(2,128)(2,1)S(1)}, bf16[8,2,1,4096]{3,2,1,0:T(2,128)(2,1)S(1)}, u32[]{:S(2)}, u32[]{:S(2)}) collective-permute-start(bf16[8,2,1,4096]{3,2,1,0:T(2,128)(2,1)S(1)} %get-tuple-element.5), channel_id=1, source_target_pairs={{4,0},{8,4},{12,8},{16,12},{20,16},{24,20},{28,24},{5,1},{9,5},{13... | collective-permute-start | bytes 393224 | tf_op jit(solution)/shard_map/ppermute | solution.py:19
  4.1 15.7 %collective-permute-start = (bf16[8,2,1,4096]{3,2,1,0:T(2,128)(2,1)S(1)}, bf16[8,2,1,4096]{3,2,1,0:T(2,128)(2,1)S(1)}, u32[]{:S(2)}, u32[]{:S(2)}) collective-permute-start(bf16[8,2,1,4096]{3,2,1,0:T(2,128)(2,1)S(1)} %get-tuple-element.6), channel_id=1, source_target_pairs={{0,4},{4,8},{8,12},{12,16},{16,20},{20,24},{24,28},{1,5},{5,9},{9,... | collective-permute-start | bytes 393224 | tf_op jit(solution)/shard_map/ppermute | solution.py:18
  9.7 4.7 %collective-permute-start.2 = (bf16[8,2,4,1]{3,2,1,0:T(4,128)(2,1)S(1)}, bf16[8,2,4,1]{3,2,1,0:T(4,128)(2,1)S(1)}, u32[]{:S(2)}, u32[]{:S(2)}) collective-permute-start(bf16[8,2,4,1]{3,2,1,0:T(4,128)(2,1)S(1)} %get-tuple-element.7), channel_id=1, source_target_pairs={{0,1},{1,2},{2,3},{3,0},{4,5},{5,6},{6,7},{7,4},{8,9},{9,10},{10,1... | collective-permute-start | bytes 392 | tf_op jit(solution)/shard_map/ppermute | solution.py:18
  9.8 1.7 %copy-start.3 = (s32[32]{0:T(128)S(1)}, s32[32]{0:T(128)}, u32[]{:S(2)}) copy-start(s32[32]{0:T(128)} %param.8) | copy-start | bytes 388
  9.8 4.6 %collective-permute-start.3 = (bf16[8,2,4,1]{3,2,1,0:T(4,128)(2,1)S(1)}, bf16[8,2,4,1]{3,2,1,0:T(4,128)(2,1)S(1)}, u32[]{:S(2)}, u32[]{:S(2)}) collective-permute-start(bf16[8,2,4,1]{3,2,1,0:T(4,128)(2,1)S(1)} %get-tuple-element.8), channel_id=1, source_target_pairs={{1,0},{2,1},{3,2},{0,3},{5,4},{6,5},{7,6},{4,7},{9,8},{10,9},{11,1... | collective-permute-start | bytes 392 | tf_op jit(solution)/shard_map/ppermute | solution.py:19
  26.6 7.0 %copy-start = (bf16[4,8,4,1024]{3,2,1,0:T(4,128)(2,1)S(1)}, bf16[4,8,4,1024]{3,2,1,0:T(4,128)(2,1)}, u32[]{:S(2)}) copy-start(bf16[4,8,4,1024]{3,2,1,0:T(4,128)(2,1)} %param.9) | copy-start | bytes 786436
  27.7 12.4 %all-to-all-start = ((f32[8,1,512]{2,1,0:T(1,128)}), f32[8,1,512]{2,1,0:T(1,128)S(1)}, u32[]{:S(2)}, u32[]{:S(2)}) async-start(f32[8,1,512]{2,1,0:T(1,128)} %reshape.175), calls=%async_computation | async-start | bytes 32768 | tf_op jit(solution)/shard_map/all_to_all | solution.py:91
where the time goes:
time: 54.1 us; the launch traced here: 53.8 us
  starting transfers between devices  14.4 us (27%)
  waiting for transfers between devices  13.7 us (25%)
  blocking collectives  10.7 us (20%)
  other arithmetic  5.17 us (10%)
  local copies, waits for them, and re-layouts  4.95 us (9%)
  matrix products  4.74 us (9%)
    psum x1, blocking collectives, local(): summed = lax.psum(spread, 'lblk')  10.7 us
    all_to_all x1, waiting for transfers between devices, local(): lax.all_to_all(partial_value, 'blk', split_axis=4, concat_axis=2, tiled=T...  6.4 us
    all_to_all x1, starting transfers between devices, local(): lax.all_to_all(partial_value, 'blk', split_axis=4, concat_axis=2, tiled=T...  5.78 us
    ppermute x2, starting transfers between devices, padded(): before = lax.ppermute(last, axis, up)  5.6 us
    ppermute x2, waiting for transfers between devices, padded(): before = lax.ppermute(last, axis, up)  5.33 us
    ppermute x2, starting transfers between devices, padded(): after = lax.ppermute(initial, axis, down)  3.01 us
    dot_general x1, matrix products, local(): jnp.dot(flat_rows, sin_table, preferred_element_type=jnp.float32)  2.29 us
    convert_element_type x1, other arithmetic, local(): smooth = (centre + DIFFUSION * total).astype(jnp.bfloat16)  2.27 us
  transfers between devices with their start and end apart: 5, of which 3 were waited for; matrix products, arithmetic and copies ran while one was open for 2% of the time, Pallas kernels for 0%

commit v1 on v0

--- a/solution.py
+++ b/solution.py
@@ -89,7 +89,7 @@
     degrees = column * degree_part + jnp.arange(degree_part, dtype=jnp.int32)
     legendre_rows = legendre.reshape(owned_count, -1, degree_part)
     spread = lax.all_to_all(partial_value, "blk", split_axis=4, concat_axis=2, tiled=True)
-    summed = lax.psum(spread, "lblk")
+    summed = jnp.sum(lax.all_gather(spread, "lblk"), axis=0)
     fourier = summed.astype(jnp.bfloat16)
     result = legendre_section(fourier, legendre_rows, my_modes, degrees)
     return result

time: 54.1 us -> 49.2 us (0.909)
  blocking collectives: 10.7 us -> 5.78 us
    psum x1 -> x0, blocking collectives: 10.7 us -> none  [local(): summed = lax.psum(spread, 'lblk')]
    all_gather x0 -> x1, blocking collectives: none -> 5.78 us  [local(): summed = jnp.sum(lax.all_gather(spread, 'lblk'), axis=0)]
where the time goes in v1:
time: 49.2 us; the launch traced here: 48.9 us
  starting transfers between devices  14.4 us (29%)
  waiting for transfers between devices  13.7 us (28%)
  blocking collectives  5.78 us (12%)
  other arithmetic  5.2 us (11%)
  local copies, waits for them, and re-layouts  4.95 us (10%)
  matrix products  4.74 us (10%)
    all_to_all x1, waiting for transfers between devices, local(): lax.all_to_all(partial_value, 'blk', split_axis=4, concat_axis=2, tiled=T...  6.4 us
    all_to_all x1, starting transfers between devices, local(): lax.all_to_all(partial_value, 'blk', split_axis=4, concat_axis=2, tiled=T...  5.78 us
    all_gather x1, blocking collectives, local(): summed = jnp.sum(lax.all_gather(spread, 'lblk'), axis=0)  5.78 us
    ppermute x2, starting transfers between devices, padded(): before = lax.ppermute(last, axis, up)  5.6 us
    ppermute x2, waiting for transfers between devices, padded(): before = lax.ppermute(last, axis, up)  5.33 us
    ppermute x2, starting transfers between devices, padded(): after = lax.ppermute(initial, axis, down)  3.01 us
    dot_general x1, matrix products, local(): jnp.dot(flat_rows, sin_table, preferred_element_type=jnp.float32)  2.29 us
    convert_element_type x1, other arithmetic, local(): smooth = (centre + DIFFUSION * total).astype(jnp.bfloat16)  2.27 us
  transfers between devices with their start and end apart: 5, of which 3 were waited for; matrix products, arithmetic and copies ran while one was open for 2% of the time, Pallas kernels for 0%

profile of v1, /device:TPU:0, one launch (start us, length us, event | category | flops | bytes accessed | tf_op | source)
XLA Modules:
  0.0 48.9 jit_solution(3487729245378203156)
XLA Ops:
  0.0 0.0 copy-start.1
  0.0 0.0 copy-start.2
  0.0 0.7 %copy-done.1 = s32[2,4]{1,0:T(2,128)S(1)} copy-done((s32[2,4]{1,0:T(2,128)S(1)}, s32[2,4]{1,0:T(2,128)}, u32[]{:S(2)}) %copy-start.1) | copy-done | bytes 56
  0.7 0.0 copy-done.2
  0.7 0.2 fusion.16
  0.9 1.3 %broadcast_select_fusion.1 = bf16[8,2,4,4096]{3,2,1,0:T(4,128)(2,1)S(1)} fusion(bf16[8,2,4,4096]{3,2,1,0:T(4,128)(2,1)} %param.5, pred[2,4,4096]{2,1,0:T(4,128)(4,1)S(1)} %fusion.16), kind=kLoop, calls=%fused_computation.20 | loop fusion | flops 262144 | bytes 1081344 | tf_op jit(solution)/shard_map/jit(_where)/select_n | solution.py:53
  2.2 0.6 %fusion.38 = (bf16[8,2,1,4096]{3,2,1,0:T(2,128)(2,1)S(1)}, bf16[8,2,1,4096]{3,2,1,0:T(2,128)(2,1)S(1)}) fusion(bf16[8,2,4,4096]{3,2,1,0:T(4,128)(2,1)S(1)} %broadcast_select_fusion.1), kind=kLoop, calls=%fused_computation.71 | loop fusion | bytes 524288 | tf_op jit(solution)/shard_map/slice | solution.py:17
  2.8 1.3 %collective-permute-start.1 = (bf16[8,2,1,4096]{3,2,1,0:T(2,128)(2,1)S(1)}, bf16[8,2,1,4096]{3,2,1,0:T(2,128)(2,1)S(1)}, u32[]{:S(2)}, u32[]{:S(2)}) collective-permute-start(bf16[8,2,1,4096]{3,2,1,0:T(2,128)(2,1)S(1)} %get-tuple-element.5), channel_id=1, source_target_pairs={{4,0},{8,4},{12,8},{16,12},{20,16},{24,20},{28,24},{5,1},{9,5},{13... | collective-permute-start | bytes 393224 | tf_op jit(solution)/shard_map/ppermute | solution.py:19
  4.1 5.5 %collective-permute-start = (bf16[8,2,1,4096]{3,2,1,0:T(2,128)(2,1)S(1)}, bf16[8,2,1,4096]{3,2,1,0:T(2,128)(2,1)S(1)}, u32[]{:S(2)}, u32[]{:S(2)}) collective-permute-start(bf16[8,2,1,4096]{3,2,1,0:T(2,128)(2,1)S(1)} %get-tuple-element.6), channel_id=1, source_target_pairs={{0,4},{4,8},{8,12},{12,16},{16,20},{20,24},{24,28},{1,5},{5,9},{9,... | collective-permute-start | bytes 393224 | tf_op jit(solution)/shard_map/ppermute | solution.py:18
  9.6 0.1 fusion.39
  9.7 0.1 collective-permute-start.2
  9.8 0.0 copy-start.3
  9.8 1.7 %collective-permute-start.3 = (bf16[8,2,4,1]{3,2,1,0:T(4,128)(2,1)S(1)}, bf16[8,2,4,1]{3,2,1,0:T(4,128)(2,1)S(1)}, u32[]{:S(2)}, u32[]{:S(2)}) collective-permute-start(bf16[8,2,4,1]{3,2,1,0:T(4,128)(2,1)S(1)} %get-tuple-element.8), channel_id=1, source_target_pairs={{1,0},{2,1},{3,2},{0,3},{5,4},{6,5},{7,6},{4,7},{9,8},{10,9},{11,1... | collective-permute-start | bytes 392 | tf_op jit(solution)/shard_map/ppermute | solution.py:19
  11.5 0.0 copy-done.3
  11.5 0.1 fusion.28
  11.6 0.3 slice.52
  11.9 0.1 dynamic_slice.3
  12.0 2.0 %collective-permute-done.1 = bf16[8,2,1,4096]{3,2,1,0:T(2,128)(2,1)S(1)} collective-permute-done((bf16[8,2,1,4096]{3,2,1,0:T(2,128)(2,1)S(1)}, bf16[8,2,1,4096]{3,2,1,0:T(2,128)(2,1)S(1)}, u32[]{:S(2)}, u32[]{:S(2)}) %collective-permute-start.1) | collective-permute-done | bytes 131104 | tf_op jit(solution)/shard_map/ppermute | solution.py:19
  14.0 0.4 broadcast_select_fusion
  14.4 0.0 collective-permute-done.2
  14.4 0.0 collective-permute-done.3
  14.4 5.3 %collective-permute-done = bf16[8,2,1,4096]{3,2,1,0:T(2,128)(2,1)S(1)} collective-permute-done((bf16[8,2,1,4096]{3,2,1,0:T(2,128)(2,1)S(1)}, bf16[8,2,1,4096]{3,2,1,0:T(2,128)(2,1)S(1)}, u32[]{:S(2)}, u32[]{:S(2)}) %collective-permute-start) | collective-permute-done | bytes 131104 | tf_op jit(solution)/shard_map/ppermute | solution.py:18
  19.7 2.3 %fusion.2 = bf16[8,2,4,4096]{3,2,1,0:T(4,128)(2,1)S(1)} fusion(bf16[8,2,4,4096]{3,2,1,0:T(4,128)(2,1)S(1)} %broadcast_select_fusion.1, bf16[8,2,4,1]{3,2,1,0:T(4,128)(2,1)S(1)} %collective-permute-done.3, bf16[8,2,4,1]{3,2,1,0:T(4,128)(2,1)S(1)} %collective-permute-done.2, bf16[8,2,1,4096]{3,2,1,0:T(2,128)(2,1)S(1)} %collective-permute-done, ...), kind=kLoop, calls=%fused_computation.5 | loop fusion | flops 6553600 | bytes 1704192 | tf_op jit(solution)/shard_map/convert_element_type | solution.py:66
  22.0 2.2 %fusion.7 = f32[8,2,4,32]{3,2,1,0:T(4,128)S(1)} fusion(bf16[8,2,4,4096]{3,2,1,0:T(4,128)(2,1)S(1)} %fusion.2, s32[32]{0:T(128)S(1)} %copy-done.3, s32[4096]{0:T(1024)S(1)} %iota_add_fusion), kind=kOutput, calls=%fused_computation.22 | convolution fusion | flops 18743296 | bytes 548992 | tf_op jit(solution)/shard_map/dot_general | solution.py:70
  24.3 2.3 %multiply_bitcast_fusion.1 = (f32[8,2,4,1,32]{4,2,1,0,3:T(4,128)S(1)}, f32[8,2,4,1,32]{4,2,1,0,3:T(4,128)S(1)}) fusion(f32[8,2,4,32]{3,2,1,0:T(4,128)S(1)} %fusion.7, f32[4,32]{1,0:T(4,128)S(1)} %get-tuple-element.16, f32[4,32]{1,0:T(4,128)S(1)} %get-tuple-element.15, bf16[8,2,4,4096]{3,2,1,0:T(4,128)(2,1)S(1)} %fusion.2, s32[32]{0:T(128)S(1)} %copy-done.3, ...), kind=kOutput, calls=%fused_computation.45 | convolution fusion | flops 18890752 | bytes 566400 | tf_op jit(solution)/shard_map/dot_general | solution.py:73
  26.6 0.0 copy-start
  26.6 0.2 copy.14
  26.8 0.9 %reshape.176 = f32[8,1,512]{2,1,0:T(1,128)} reshape(f32[32,2,2,4,8]{4,3,2,1,0:T(4,128)S(1)} %bitcast.33) | data formatting | bytes 32768
  27.7 5.8 %all-to-all-start = ((f32[8,1,512]{2,1,0:T(1,128)}), f32[8,1,512]{2,1,0:T(1,128)S(1)}, u32[]{:S(2)}, u32[]{:S(2)}) async-start(f32[8,1,512]{2,1,0:T(1,128)} %reshape.176), calls=%async_computation | async-start | bytes 32768 | tf_op jit(solution)/shard_map/all_to_all | solution.py:91
  33.5 0.1 broadcast_compare_fusion
  33.6 0.0 copy-done
  33.6 0.1 reshape.174
  33.6 6.4 %all-to-all-done = f32[8,1,512]{2,1,0:T(1,128)S(1)} async-done(((f32[8,1,512]{2,1,0:T(1,128)}), f32[8,1,512]{2,1,0:T(1,128)S(1)}, u32[]{:S(2)}, u32[]{:S(2)}) %all-to-all-start) | async-done | bytes 16416 | tf_op jit(solution)/shard_map/all_to_all | solution.py:91
  40.0 0.5 %broadcast.207 = f32[]{:T(128)} broadcast(f32[]{:T(128)} %constant.147), dimensions={} | broadcast | bytes 8 | tf_op jit(solution)/shard_map/all_to_all | solution.py:91
  40.5 0.7 %reduce = f32[8,512]{1,0:T(8,128)S(1)} reduce(f32[8,1,512]{2,1,0:T(1,128)S(1)} %all-to-all-done, f32[]{:T(128)} %broadcast.207), dimensions={1}, to_apply=%all_to_all.11.reduce_sub_computation | reduce | bytes 32772 | tf_op jit(solution)/shard_map/all_to_all | solution.py:91
  41.2 0.3 reshape.177
  41.6 0.1 copy.15
  41.7 0.2 copy.16
  41.9 0.1 copy.17
  42.0 5.8 %all_gather.7 = f32[4,8,2,32,2,4]{3,1,5,4,2,0:T(8,128)S(1)} all-gather(f32[1,8,2,32,2,4]{3,1,5,4,2,0:T(8,128)S(1)} %copy.17), channel_id=1, replica_groups=mesh['blk'=8,'lblk'=4] {'lblk'}, dimensions={0}, use_global_device_ids=true | all-gather | bytes 81920 | tf_op jit(solution)/shard_map/all_gather | solution.py:92
  47.8 0.2 convolution_bitcast_fusion
  48.0 0.1 fusion.12
  48.1 0.9 %copy.20 = f32[8,2,4,1024]{3,2,1,0:T(4,128)} copy(f32[8,2,4,1024]{3,0,1,2:T(8,128)S(1)} %fusion.12) | data formatting | bytes 524288 | tf_op jit(solution)/shard_map/jit(_where)/select_n | solution.py:42
  (6 shorter events, 0.1 us)
Async XLA Ops:
  0.0 0.7 %copy-start.1 = (s32[2,4]{1,0:T(2,128)S(1)}, s32[2,4]{1,0:T(2,128)}, u32[]{:S(2)}) copy-start(s32[2,4]{1,0:T(2,128)} %param.7) | copy-start | bytes 100
  0.0 0.7 %copy-start.2 = (s32[2,4]{1,0:T(2,128)S(1)}, s32[2,4]{1,0:T(2,128)}, u32[]{:S(2)}) copy-start(s32[2,4]{1,0:T(2,128)} %param.6) | copy-start | bytes 100
  2.8 11.2 %collective-permute-start.1 = (bf16[8,2,1,4096]{3,2,1,0:T(2,128)(2,1)S(1)}, bf16[8,2,1,4096]{3,2,1,0:T(2,128)(2,1)S(1)}, u32[]{:S(2)}, u32[]{:S(2)}) collective-permute-start(bf16[8,2,1,4096]{3,2,1,0:T(2,128)(2,1)S(1)} %get-tuple-element.5), channel_id=1, source_target_pairs={{4,0},{8,4},{12,8},{16,12},{20,16},{24,20},{28,24},{5,1},{9,5},{13... | collective-permute-start | bytes 393224 | tf_op jit(solution)/shard_map/ppermute | solution.py:19
  4.1 15.7 %collective-permute-start = (bf16[8,2,1,4096]{3,2,1,0:T(2,128)(2,1)S(1)}, bf16[8,2,1,4096]{3,2,1,0:T(2,128)(2,1)S(1)}, u32[]{:S(2)}, u32[]{:S(2)}) collective-permute-start(bf16[8,2,1,4096]{3,2,1,0:T(2,128)(2,1)S(1)} %get-tuple-element.6), channel_id=1, source_target_pairs={{0,4},{4,8},{8,12},{12,16},{16,20},{20,24},{24,28},{1,5},{5,9},{9,... | collective-permute-start | bytes 393224 | tf_op jit(solution)/shard_map/ppermute | solution.py:18
  9.7 4.7 %collective-permute-start.2 = (bf16[8,2,4,1]{3,2,1,0:T(4,128)(2,1)S(1)}, bf16[8,2,4,1]{3,2,1,0:T(4,128)(2,1)S(1)}, u32[]{:S(2)}, u32[]{:S(2)}) collective-permute-start(bf16[8,2,4,1]{3,2,1,0:T(4,128)(2,1)S(1)} %get-tuple-element.7), channel_id=1, source_target_pairs={{0,1},{1,2},{2,3},{3,0},{4,5},{5,6},{6,7},{7,4},{8,9},{9,10},{10,1... | collective-permute-start | bytes 392 | tf_op jit(solution)/shard_map/ppermute | solution.py:18
  9.8 1.7 %copy-start.3 = (s32[32]{0:T(128)S(1)}, s32[32]{0:T(128)}, u32[]{:S(2)}) copy-start(s32[32]{0:T(128)} %param.8) | copy-start | bytes 388
  9.8 4.6 %collective-permute-start.3 = (bf16[8,2,4,1]{3,2,1,0:T(4,128)(2,1)S(1)}, bf16[8,2,4,1]{3,2,1,0:T(4,128)(2,1)S(1)}, u32[]{:S(2)}, u32[]{:S(2)}) collective-permute-start(bf16[8,2,4,1]{3,2,1,0:T(4,128)(2,1)S(1)} %get-tuple-element.8), channel_id=1, source_target_pairs={{1,0},{2,1},{3,2},{0,3},{5,4},{6,5},{7,6},{4,7},{9,8},{10,9},{11,1... | collective-permute-start | bytes 392 | tf_op jit(solution)/shard_map/ppermute | solution.py:19
  26.6 7.0 %copy-start = (bf16[4,8,4,1024]{3,2,1,0:T(4,128)(2,1)S(1)}, bf16[4,8,4,1024]{3,2,1,0:T(4,128)(2,1)}, u32[]{:S(2)}) copy-start(bf16[4,8,4,1024]{3,2,1,0:T(4,128)(2,1)} %param.9) | copy-start | bytes 786436
  27.7 12.4 %all-to-all-start = ((f32[8,1,512]{2,1,0:T(1,128)}), f32[8,1,512]{2,1,0:T(1,128)S(1)}, u32[]{:S(2)}, u32[]{:S(2)}) async-start(f32[8,1,512]{2,1,0:T(1,128)} %reshape.176), calls=%async_computation | async-start | bytes 32768 | tf_op jit(solution)/shard_map/all_to_all | solution.py:91
